TPU v7x, 256 devices: a whole 4x4x8 slice. The times are simulated.
256 devices in a mesh: basin: 32 (over y, x, core), tm: 8 (over z).
Axes of the slice: x: 4, y: 4, z: 8, core: 2. Of those that a mesh axis runs over, the one named last changes fastest.
Arguments:
- inflow: float32 [256, 131072], P('tm', 'basin'), may hold values from 0.01 to 0.1
- cotangent: float32 [256, 65536], P('tm', 'basin'), may hold values from -6 to 6
- gauge_reach: int32 [65536], P('basin'), may hold values from 0 to 4095
- shape_param: float32 [131072], P('basin'), may hold values from 1.5 to 4
- scale_param: float32 [131072], P('basin'), may hold values from 1.5 to 10
- block_level: int32 [512], P('basin'), may hold values from 0 to 7, as said below
- down_local: int32 [131072], P('basin'), may hold values from -1 to 4095, as said below
- in_slot: int32 [131072], P('basin'), may hold values from -1 to 127, as said below
- send_reach: int32 [32, 7, 128], P('basin'), may hold values from -1 to 4095, as said below
Outputs:
- lateral_grad: float32 [256, 131072], P('tm', 'basin')
- param_grad: float32 [2, 131072], P(None, 'basin')
Inputs may be any that keep to these rules, and one draw needn't show every extreme that they name: `block_level`: every partition holds between one and 4 blocks of each level, and exactly 4 blocks of some level. `down_local`: for a reach in a block of level h >= 1 whose in_slot is -1: a reach of the same partition in a block of level h - 1. -1 for reaches of level 0 and for reaches with in_slot >= 0. `in_slot`: A value s * 4 + c (s a partition other than the reach's own, c < 4) marks a reach of level h >= 1 fed by slot c that partition s fills for it at level h - 1; within one partition no value repeats among the reaches of one level. Exactly the slots that send_reach fills are received. send_reach[s, h, t * 4 + c] is a reach of partition s in a block of level h, or -1 for an empty slot; slots with t = s are empty. At some level some partition t receives all 4 slots from every other partition.
All inputs are finite; a program needn't handle non-finite values.
Results may differ from a plain program's by a relative error of at most 0.0003.
Values sent between devices are 32-bit elements; how exact they have to be, the bound alone decides.
A program may use at most 128 MiB of HBM per device.

v0:
```python
import functools
import math

import jax
import jax.numpy as jnp
from jax import lax
from jax.experimental import pallas as pl
from jax.experimental.pallas import tpu as pltpu
from jax.sharding import PartitionSpec as P

BLK = 256
LAGS = 30
LEVELS = 8
MAXB = 4
CAP = 4
LANES = 128
TILES = MAXB * BLK // LANES
HALO = LAGS - 1
OFFSETS = [k + 0.5 for k in range(LAGS)]
LOGS = [math.log(o) for o in OFFSETS]


def block_tables(block_level):
    ids = jnp.arange(block_level.shape[0], dtype=jnp.int32)
    before = (block_level[None, :] == block_level[:, None]) & (ids[None, :] < ids[:, None])
    place = block_level * MAXB + jnp.sum(before.astype(jnp.int32), axis=1)
    slots = jnp.arange(LEVELS * MAXB, dtype=jnp.int32)
    order = jnp.sum(jnp.where(place[None, :] == slots[:, None], ids[None, :], 0), axis=1)
    return jnp.concatenate([order, place])


def adjoint_kernel(
    parts,
    shifts,
    days,
    table,
    cot,
    gauge,
    inflow,
    shape_p,
    scale_p,
    down,
    inslot,
    send,
    lat,
    par,
    cot2,
    gpos,
    seed,
    infl,
    kern,
    dlane,
    dtile,
    rlane,
    wlane,
    wtile,
    scl_lv,
    adj,
    lday,
    xsend,
    xrecv,
    out_msg,
    own_msg,
    far_msg,
    turn,
    rows_own,
    rows_far,
    lag_sum,
    psend,
    precv,
    ptotal,
    lat_lv,
    staged,
    sx,
    rx,
    so,
    sf,
    ro,
    rf,
    sp,
    rp,
):
    blocks = inflow.shape[1] // BLK
    me = lax.axis_index("basin")
    shift = lax.axis_index("tm")
    prev = lax.rem(shift + shifts - 1, shifts)
    has_next = shift < shifts - 1

    def tile_of(reach):
        block = reach >> 8
        slot = jnp.zeros_like(reach)
        for b in range(blocks):
            slot = jnp.where(block == b, table[LEVELS * MAXB + b], slot)
        return slot, (slot & (MAXB - 1)) * 2 + ((reach >> 7) & 1)

    def prepare(h):
        spots = [table[h * MAXB + m] * 2 + j for m in range(MAXB) for j in range(2)]

        def tiled(ref):
            return jnp.concatenate([ref[pl.ds(i, 1), :] for i in spots], axis=0)

        target = tiled(down)
        dtile[h] = jnp.where(target >= 0, tile_of(target)[1], -1)
        dlane[h] = target & (LANES - 1)
        rlane[h] = tiled(inslot)
        shp = tiled(shape_p) - 1.0
        scl = tiled(scale_p)
        scl_lv[h] = scl
        weights = [jnp.exp(shp * LOGS[k] - OFFSETS[k] / scl) for k in range(LAGS)]
        total = weights[0]
        for k in range(1, LAGS):
            total = total + weights[k]
        for k in range(LAGS):
            kern[h, k] = weights[k] / total

    def seeds(h):
        width = 2 * LANES
        local = gpos[...] - h * (MAXB * BLK)

        ids = lax.broadcasted_iota(jnp.int32, (width, local.shape[1]), 0)
        for c in range(MAXB * BLK // width):
            hot = jnp.where(ids == local - c * width, 1.0, 0.0).astype(jnp.bfloat16)
            both = lax.dot_general(
                cot2[...], hot, (((1,), (1,)), ((), ())), preferred_element_type=jnp.float32
            )
            sums = both[:days] + both[days:]
            for j in range(width // LANES):
                seed[h, :, 2 * c + j, :] = sums[:, j * LANES : (j + 1) * LANES]

    def routed(h):
        total = kern[h, 0][None] * adj[pl.ds(0, days)]
        for k in range(1, LAGS):
            total = total + kern[h, k][None] * adj[pl.ds(k, days)]
        lday[...] = total

    def outgoing(h):
        lane, tile = wlane[h], wtile[h]
        for g in range(days // 8):
            picked = jnp.zeros((8, LANES), jnp.float32)
            for s in range(TILES):
                got = jnp.take_along_axis(lday[pl.ds(8 * g, 8), s, :], lane, axis=1)
                picked = jnp.where(tile == s, got, picked)
            turn[0, 8 * g : 8 * g + 8, :] = picked
        turn[0] = jnp.transpose(turn[0])
        lanes = lax.broadcasted_iota(jnp.int32, (parts, LANES), 1)
        packed = jnp.zeros((parts, LANES), jnp.float32)
        for c in range(CAP):
            piece = turn[0, pl.ds(c, parts, stride=CAP), :]
            piece = pltpu.roll(piece, c * days, axis=1) if c else piece
            packed = jnp.where((lanes >= c * days) & (lanes < (c + 1) * days), piece, packed)
        out_msg[h, :, 0, :] = packed

    def slot_copy(h, q, target, ssem, buf, rsem):
        return pltpu.make_async_remote_copy(
            src_ref=out_msg.at[h, q],
            dst_ref=buf.at[h, me],
            send_sem=ssem.at[h],
            recv_sem=rsem.at[h],
            device_id={"basin": q, "tm": target},
            device_id_type=pl.DeviceIdType.MESH,
        )

    def send_slots(h):
        @pl.loop(1, parts)
        def _(i):
            q = lax.rem(me + i, parts)
            slot_copy(h, q, prev, sf, far_msg, rf).start()
            slot_copy(h, q, shift, so, own_msg, ro).start()

    def local_part(h):
        lane, tile = dlane[h], dtile[h]
        masks = [tile == s for s in range(TILES)]

        @pl.loop(0, days, unroll=4)
        def _(t):
            got = jnp.zeros((TILES, LANES), jnp.float32)
            for s in range(TILES):
                line = jnp.broadcast_to(lday[t, s : s + 1, :], (TILES, LANES))
                got = jnp.where(masks[s], jnp.take_along_axis(line, lane, axis=1), got)
            xsend[h, t] = seed[h, t] + got

    def halo_copy(h):
        return pltpu.make_async_remote_copy(
            src_ref=xsend.at[h, pl.ds(0, HALO)],
            dst_ref=xrecv.at[h],
            send_sem=sx.at[h],
            recv_sem=rx.at[h],
            device_id={"basin": me, "tm": prev},
            device_id_type=pl.DeviceIdType.MESH,
        )

    def unpack(h, buf, rows):
        arrived = buf[h, :, 0, :]
        for c in range(CAP):
            piece = pltpu.roll(arrived, LANES - c * days, axis=1) if c else arrived
            turn[1, pl.ds(c, parts, stride=CAP), :] = piece
        rows[...] = jnp.transpose(turn[1])[: rows.shape[0]]

    def remote_part(h, row):
        slot = rlane[h]
        line = jnp.broadcast_to(row, (TILES, LANES))
        got = jnp.take_along_axis(line, slot & (LANES - 1), axis=1)
        return jnp.where(slot >= 0, got, 0.0)

    def gradient(h):
        for m in range(MAXB):
            block = table[h * MAXB + m]
            for j in range(2):
                infl[:, 2 * m + j, :] = staged[block * 2 + j]
        for k in range(LAGS):
            lag_sum[k] = jnp.sum(infl[...] * adj[pl.ds(k, days)], axis=0)
        mean = kern[h, 0] * lag_sum[0]
        for k in range(1, LAGS):
            mean = mean + kern[h, k] * lag_sum[k]
        first = jnp.zeros((TILES, LANES), jnp.float32)
        second = jnp.zeros((TILES, LANES), jnp.float32)
        for k in range(LAGS):
            logit = kern[h, k] * (lag_sum[k] - mean)
            first = first + logit * LOGS[k]
            second = second + logit * OFFSETS[k]
        scl = scl_lv[h]
        psend[h, 0] = first
        psend[h, 1] = second / (scl * scl)

    def grad_copy(h, i):
        return pltpu.make_async_remote_copy(
            src_ref=psend.at[h],
            dst_ref=precv.at[h, i - 1],
            send_sem=sp.at[h],
            recv_sem=rp.at[h],
            device_id={"basin": me, "tm": lax.rem(shift + i, shifts)},
            device_id_type=pl.DeviceIdType.MESH,
        )

    def send_grads(h):
        for i in range(1, shifts):
            grad_copy(h, i).start()

    def keep(h):
        for s in range(TILES):
            lat_lv[h * TILES + s] = lday[:, s, :]

    def wait_bytes(ref, sem):
        pltpu.make_async_copy(ref, ref, sem).wait()

    value = cot[...]
    high = value.astype(jnp.bfloat16)
    cot2[pl.ds(0, days), :] = high
    cot2[pl.ds(days, days), :] = (value - high.astype(jnp.float32)).astype(jnp.bfloat16)
    reach = gauge[...]
    gpos[...] = tile_of(reach)[0] * BLK + (reach & (BLK - 1))
    seeds(0)
    xsend[0] = seed[0]
    halo_copy(0).start()
    wanted = jnp.maximum(send[...], 0)
    wanted_tile = tile_of(wanted)[1]
    for h in range(LEVELS - 1):
        wlane[h] = jnp.broadcast_to(wanted[h : h + 1, :] & (LANES - 1), (8, LANES))
        wtile[h] = jnp.broadcast_to(wanted_tile[h : h + 1, :], (8, LANES))
    turn[...] = jnp.zeros_like(turn)
    for i in range(2 * blocks):
        staged[i] = inflow[:, i * LANES : (i + 1) * LANES]
    prepare(0)
    prepare(1)
    seeds(1)
    halo_copy(0).wait_recv()
    adj[pl.ds(0, days)] = xsend[0]
    adj[pl.ds(days, HALO)] = jnp.where(has_next, xrecv[0], 0.0)

    @pl.loop(0, LEVELS - 1)
    def _(h):
        routed(h)
        outgoing(h)
        send_slots(h)
        local_part(h + 1)
        halo_copy(h + 1).start()
        gradient(h)
        send_grads(h)
        keep(h)

        @pl.when(h < LEVELS - 2)
        def _():
            seeds(h + 2)

        prepare(jnp.minimum(h + 2, LEVELS - 1))
        wait_bytes(own_msg.at[h, pl.ds(0, parts - 1)], ro.at[h])
        unpack(h, own_msg, rows_own)
        for t in range(days):
            adj[t] = xsend[h + 1, t] + remote_part(h + 1, rows_own[t : t + 1, :])
        wait_bytes(far_msg.at[h, pl.ds(0, parts - 1)], rf.at[h])
        unpack(h, far_msg, rows_far)
        halo_copy(h + 1).wait_recv()
        for t in range(HALO):
            value = xrecv[h + 1, t] + remote_part(h + 1, rows_far[t : t + 1, :])
            adj[days + t] = jnp.where(has_next, value, 0.0)

    last = LEVELS - 1
    gradient(last)
    send_grads(last)
    routed(last)
    keep(last)
    for b in range(blocks):
        place = table[LEVELS * MAXB + b]
        for j in range(2):
            lat[:, pl.ds(b * BLK + j * LANES, LANES)] = lat_lv[place * 2 + j]

    @pl.loop(0, LEVELS)
    def _(h):
        wait_bytes(precv.at[h], rp.at[h])
        total = psend[h]
        for i in range(shifts - 1):
            total = total + precv[h, i]
        for r in range(2):
            ptotal[r, pl.ds(pl.multiple_of(h * TILES, TILES), TILES), :] = total[r]

    for b in range(blocks):
        place = table[LEVELS * MAXB + b]
        for j in range(2):
            for r in range(2):
                line = ptotal[r, pl.ds(place * 2 + j, 1), :]
                par[r : r + 1, pl.ds(b * BLK + j * LANES, LANES)] = line

    @pl.loop(0, LEVELS)
    def _(h):
        wait_bytes(xsend.at[h, pl.ds(0, HALO)], sx.at[h])
        wait_bytes(precv.at[h], sp.at[h])

    @pl.loop(0, LEVELS - 1)
    def _(h):
        wait_bytes(out_msg.at[h, pl.ds(0, parts - 1)], so.at[h])
        wait_bytes(out_msg.at[h, pl.ds(0, parts - 1)], sf.at[h])


def shards(parts, shifts, inflow, cotangent, gauge_reach, shape_param, scale_param, block_level, down_local, in_slot, send_reach):
    days, reaches = inflow.shape
    gauges = cotangent.shape[1]
    lines = reaches // LANES
    send = send_reach[0]
    if send.shape[1] < LANES:
        send = jnp.pad(send, ((0, 0), (0, LANES - send.shape[1])))
    f32, i32 = jnp.float32, jnp.int32
    levels = LEVELS
    rounds = LEVELS - 1
    tile = (TILES, LANES)
    vmem = pl.BlockSpec(memory_space=pltpu.VMEM)
    dma = pltpu.SemaphoreType.DMA
    return pl.pallas_call(
        functools.partial(adjoint_kernel, parts, shifts, days),
        out_shape=(
            jax.ShapeDtypeStruct((days, reaches), f32),
            jax.ShapeDtypeStruct((2, reaches), f32),
        ),
        in_specs=[pl.BlockSpec(memory_space=pltpu.SMEM)] + [vmem] * 8,
        out_specs=(vmem, vmem),
        scratch_shapes=[
            pltpu.VMEM((2 * days, gauges), jnp.bfloat16),
            pltpu.VMEM((1, gauges), i32),
            pltpu.VMEM((levels, days) + tile, f32),
            pltpu.VMEM((days,) + tile, f32),
            pltpu.VMEM((levels, LAGS) + tile, f32),
            pltpu.VMEM((levels,) + tile, i32),
            pltpu.VMEM((levels,) + tile, i32),
            pltpu.VMEM((levels,) + tile, i32),
            pltpu.VMEM((rounds,) + tile, i32),
            pltpu.VMEM((rounds,) + tile, i32),
            pltpu.VMEM((levels,) + tile, f32),
            pltpu.VMEM((days + HALO,) + tile, f32),
            pltpu.VMEM((days,) + tile, f32),
            pltpu.VMEM((levels, days) + tile, f32),
            pltpu.VMEM((levels, HALO) + tile, f32),
            pltpu.VMEM((rounds, parts, 1, LANES), f32),
            pltpu.VMEM((rounds, parts, 1, LANES), f32),
            pltpu.VMEM((rounds, parts, 1, LANES), f32),
            pltpu.VMEM((2, LANES, LANES), f32),
            pltpu.VMEM((days, LANES), f32),
            pltpu.VMEM((days, LANES), f32),
            pltpu.VMEM((LAGS,) + tile, f32),
            pltpu.VMEM((levels, 2) + tile, f32),
            pltpu.VMEM((levels, shifts - 1, 2) + tile, f32),
            pltpu.VMEM((2, levels * TILES, LANES), f32),
            pltpu.VMEM((levels * TILES, days, LANES), f32),
            pltpu.VMEM((lines, days, LANES), f32),
            dma((levels,)),
            dma((levels,)),
            dma((rounds,)),
            dma((rounds,)),
            dma((rounds,)),
            dma((rounds,)),
            dma((levels,)),
            dma((levels,)),
        ],
        compiler_params=pltpu.CompilerParams(
            has_side_effects=True, vmem_limit_bytes=40 * 1024 * 1024
        ),
    )(
        block_tables(block_level),
        cotangent,
        gauge_reach.reshape(1, gauges),
        inflow,
        shape_param.reshape(lines, LANES),
        scale_param.reshape(lines, LANES),
        down_local.reshape(lines, LANES),
        in_slot.reshape(lines, LANES),
        send,
    )


def solution(mesh):
    in_specs = (
        P("tm", "basin"),
        P("tm", "basin"),
        P("basin"),
        P("basin"),
        P("basin"),
        P("basin"),
        P("basin"),
        P("basin"),
        P("basin", None, None),
    )
    out_specs = (P("tm", "basin"), P(None, "basin"))
    body = functools.partial(shards, mesh.shape["basin"], mesh.shape["tm"])
    return jax.shard_map(body, mesh=mesh, in_specs=in_specs, out_specs=out_specs, check_vma=False)
```

profile of v0, /device:TPU:1, one launch (start us, length us, event | category | flops | bytes accessed | tf_op | source)
XLA Modules:
  0.0 87.6 jit_solution(5733731195245336744)
XLA Ops:
  0.6 0.0 copy-start.2
  0.6 0.9 %convert_reduce_fusion = s32[16]{0:T(128)S(1)} fusion(s32[16]{0:T(128)} %param.14), kind=kLoop, calls=%fused_computation.2 | loop fusion | flops 1264 | bytes 128 | tf_op jit(solution)/shard_map/reduce_sum | solution.py:26
  1.6 0.0 copy-start.6
  1.6 0.7 multiply_add_fusion
  2.2 0.1 select_reduce_fusion
  2.3 0.1 pad_add_fusion.table
  2.4 0.7 copy.13
  3.1 0.0 copy-done.2
  3.1 0.0 copy-done.6
  3.1 0.0 copy-start
  3.1 1.0 %copy-done = f32[32,4096]{1,0:T(8,128)S(1)} copy-done((f32[32,4096]{1,0:T(8,128)S(1)}, f32[32,4096]{1,0:T(8,128)}, u32[]{:S(2)}) %copy-start) | copy-done | bytes 524312
  4.1 0.0 copy-start.1
  4.1 0.9 %copy-done.1 = f32[32,2048]{1,0:T(8,128)S(1)} copy-done((f32[32,2048]{1,0:T(8,128)S(1)}, f32[32,2048]{1,0:T(8,128)}, u32[]{:S(2)}) %copy-start.1) | copy-done | bytes 262168
  5.1 0.0 copy-start.3
  5.1 0.7 copy-done.3
  5.8 0.0 copy-start.4
  5.8 0.7 copy-done.4
  6.5 0.0 copy-start.5
  6.5 0.7 copy-done.5
  7.2 78.9 %shard_map.104 = (f32[32,4096]{1,0:T(8,128)S(1)}, f32[2,4096]{1,0:T(2,128)S(1)}) custom-call(s32[48]{0:T(128)S(1)} %pad_add_fusion.table, f32[32,2048]{1,0:T(8,128)S(1)} %copy-done.1, s32[1,2048]{1,0:T(1,128)S(1)} %bitcast.13, f32[32,4096]{1,0:T(8,128)S(1)} %copy-done, f32[32,128]{1,0:T(8,128)S(1)} %bitcast.9, f32[32,128]{1,0:T(8,128)S(1)} %bitcast.10, ...), custom_call_target="tpu_custom_call" | custom-call | tf_op jit(solution)/shard_map/pallas_call | solution.py:347
  86.2 0.8 copy.16
  87.0 0.6 copy.17
Async XLA Ops:
  0.6 2.5 %copy-start.2 = (f32[4096]{0:T(1024)S(1)}, f32[4096]{0:T(1024)}, u32[]{:S(2)}) copy-start(f32[4096]{0:T(1024)} %param.12) | copy-start | bytes 49156
  1.6 1.5 %copy-start.6 = (s32[2048]{0:T(1024)S(1)}, s32[2048]{0:T(1024)}, u32[]{:S(2)}) copy-start(s32[2048]{0:T(1024)} %param.11) | copy-start | bytes 24580
  3.1 1.0 %copy-start = (f32[32,4096]{1,0:T(8,128)S(1)}, f32[32,4096]{1,0:T(8,128)}, u32[]{:S(2)}) copy-start(f32[32,4096]{1,0:T(8,128)} %inflow.1) | copy-start | bytes 1572868
  4.1 0.9 %copy-start.1 = (f32[32,2048]{1,0:T(8,128)S(1)}, f32[32,2048]{1,0:T(8,128)}, u32[]{:S(2)}) copy-start(f32[32,2048]{1,0:T(8,128)} %cot.1) | copy-start | bytes 786436
  5.1 0.7 copy-start.3
  5.8 0.7 copy-start.4
  6.5 0.7 copy-start.5
where the time goes:
time: 88.2 us; the launch traced here: 87.6 us
  Pallas kernels  78.9 us (89%)
  local copies, waits for them, and re-layouts  6.25 us (7%)
  other arithmetic  1.75 us (2%)
    pallas_call x1, Pallas kernels, shards(): pl.pallas_call(functools.partial(adjoint_kernel, parts, shifts, days), ou...  78.9 us
    unnamed x17, local copies, waits for them, and re-layouts  6.25 us

commit v1 on v0

--- a/solution.py
+++ b/solution.py
@@ -16,34 +16,35 @@
 LANES = 128
 TILES = MAXB * BLK // LANES
 HALO = LAGS - 1
+UNROLL = 32
 OFFSETS = [k + 0.5 for k in range(LAGS)]
 LOGS = [math.log(o) for o in OFFSETS]
-
-
-def block_tables(block_level):
-    ids = jnp.arange(block_level.shape[0], dtype=jnp.int32)
-    before = (block_level[None, :] == block_level[:, None]) & (ids[None, :] < ids[:, None])
-    place = block_level * MAXB + jnp.sum(before.astype(jnp.int32), axis=1)
-    slots = jnp.arange(LEVELS * MAXB, dtype=jnp.int32)
-    order = jnp.sum(jnp.where(place[None, :] == slots[:, None], ids[None, :], 0), axis=1)
-    return jnp.concatenate([order, place])
 
 
 def adjoint_kernel(
     parts,
     shifts,
     days,
+    levels,
+    cot_h,
+    gauge_h,
+    inflow_h,
+    shape_h,
+    scale_h,
+    down_h,
+    inslot_h,
+    send_h,
+    lat,
+    par,
     table,
     cot,
     gauge,
-    inflow,
     shape_p,
     scale_p,
     down,
     inslot,
     send,
-    lat,
-    par,
+    load_sem,
     cot2,
     gpos,
     seed,
@@ -80,11 +81,12 @@
     sp,
     rp,
 ):
-    blocks = inflow.shape[1] // BLK
+    blocks = levels.shape[0]
     me = lax.axis_index("basin")
     shift = lax.axis_index("tm")
     prev = lax.rem(shift + shifts - 1, shifts)
     has_next = shift < shifts - 1
+    has_prev = shift > 0
 
     def tile_of(reach):
         block = reach >> 8
@@ -164,14 +166,20 @@
         @pl.loop(1, parts)
         def _(i):
             q = lax.rem(me + i, parts)
-            slot_copy(h, q, prev, sf, far_msg, rf).start()
             slot_copy(h, q, shift, so, own_msg, ro).start()
+
+        @pl.when(has_prev)
+        def _():
+            @pl.loop(1, parts)
+            def _(i):
+                q = lax.rem(me + i, parts)
+                slot_copy(h, q, prev, sf, far_msg, rf).start()
 
     def local_part(h):
         lane, tile = dlane[h], dtile[h]
         masks = [tile == s for s in range(TILES)]
 
-        @pl.loop(0, days, unroll=4)
+        @pl.loop(0, days, unroll=UNROLL)
         def _(t):
             got = jnp.zeros((TILES, LANES), jnp.float32)
             for s in range(TILES):
@@ -188,6 +196,16 @@
             device_id={"basin": me, "tm": prev},
             device_id_type=pl.DeviceIdType.MESH,
         )
+
+    def send_halo(h):
+        @pl.when(has_prev)
+        def _():
+            halo_copy(h).start()
+
+    def take_halo(h):
+        @pl.when(has_next)
+        def _():
+            halo_copy(h).wait_recv()
 
     def unpack(h, buf, rows):
         arrived = buf[h, :, 0, :]
@@ -243,29 +261,95 @@
     def wait_bytes(ref, sem):
         pltpu.make_async_copy(ref, ref, sem).wait()
 
+    barrier = pltpu.get_barrier_semaphore()
+
+    def greet(q, k):
+        where = {"basin": q, "tm": k}
+        pl.semaphore_signal(barrier, inc=1, device_id=where, device_id_type=pl.DeviceIdType.MESH)
+
+    loads = [
+        pltpu.make_async_copy(src, dst, load_sem.at[i])
+        for i, (src, dst) in enumerate(
+            [(cot_h, cot), (gauge_h, gauge), (shape_h, shape_p), (scale_h, scale_p), (down_h, down), (inslot_h, inslot), (send_h, send)]
+        )
+    ]
+    for copy in loads:
+        copy.start()
+    for i in range(2 * blocks):
+        pltpu.make_async_copy(
+            inflow_h.at[:, pl.ds(i * LANES, LANES)], staged.at[i], load_sem.at[len(loads)]
+        ).start()
+
+    @pl.loop(1, parts)
+    def _(i):
+        greet(lax.rem(me + i, parts), shift)
+
+    @pl.when(has_prev)
+    def _():
+        @pl.loop(0, parts)
+        def _(i):
+            greet(lax.rem(me + i, parts), prev)
+
+    @pl.when(has_next)
+    def _():
+        @pl.loop(0, parts)
+        def _(i):
+            greet(lax.rem(me + i, parts), shift + 1)
+
+    for i in range(1, shifts):
+        greet(me, lax.rem(shift + i, shifts))
+
+    level_of = [levels[b] for b in range(blocks)]
+    places = []
+    for b in range(blocks):
+        place = level_of[b] * MAXB
+        for a in range(b):
+            place = place + jnp.where(level_of[a] == level_of[b], 1, 0)
+        places.append(place)
+        table[LEVELS * MAXB + b] = place
+
+    @pl.loop(0, LEVELS * MAXB)
+    def _(i):
+        block = jnp.int32(0)
+        for b in range(1, blocks):
+            block = block + jnp.where(places[b] == i, b, 0)
+        table[i] = block
+
+    loads[0].wait()
+    loads[1].wait()
     value = cot[...]
     high = value.astype(jnp.bfloat16)
     cot2[pl.ds(0, days), :] = high
     cot2[pl.ds(days, days), :] = (value - high.astype(jnp.float32)).astype(jnp.bfloat16)
     reach = gauge[...]
     gpos[...] = tile_of(reach)[0] * BLK + (reach & (BLK - 1))
+
+    @pl.when(shift == shifts - 1)
+    def _():
+        xrecv[0] = jnp.zeros_like(xrecv[0])
+        adj[pl.ds(days, HALO)] = jnp.zeros((HALO, TILES, LANES), jnp.float32)
+
     seeds(0)
     xsend[0] = seed[0]
-    halo_copy(0).start()
+    greeted = parts - 1 + shifts - 1
+    greeted = greeted + parts * (has_prev.astype(jnp.int32) + has_next.astype(jnp.int32))
+    pl.semaphore_wait(barrier, greeted)
+    send_halo(0)
+    for copy in loads[2:]:
+        copy.wait()
     wanted = jnp.maximum(send[...], 0)
     wanted_tile = tile_of(wanted)[1]
     for h in range(LEVELS - 1):
         wlane[h] = jnp.broadcast_to(wanted[h : h + 1, :] & (LANES - 1), (8, LANES))
         wtile[h] = jnp.broadcast_to(wanted_tile[h : h + 1, :], (8, LANES))
     turn[...] = jnp.zeros_like(turn)
-    for i in range(2 * blocks):
-        staged[i] = inflow[:, i * LANES : (i + 1) * LANES]
+    pltpu.make_async_copy(staged, staged, load_sem.at[len(loads)]).wait()
     prepare(0)
     prepare(1)
     seeds(1)
-    halo_copy(0).wait_recv()
+    take_halo(0)
     adj[pl.ds(0, days)] = xsend[0]
-    adj[pl.ds(days, HALO)] = jnp.where(has_next, xrecv[0], 0.0)
+    adj[pl.ds(days, HALO)] = xrecv[0]
 
     @pl.loop(0, LEVELS - 1)
     def _(h):
@@ -273,7 +357,7 @@
         outgoing(h)
         send_slots(h)
         local_part(h + 1)
-        halo_copy(h + 1).start()
+        send_halo(h + 1)
         gradient(h)
         send_grads(h)
         keep(h)
@@ -287,12 +371,14 @@
         unpack(h, own_msg, rows_own)
         for t in range(days):
             adj[t] = xsend[h + 1, t] + remote_part(h + 1, rows_own[t : t + 1, :])
-        wait_bytes(far_msg.at[h, pl.ds(0, parts - 1)], rf.at[h])
-        unpack(h, far_msg, rows_far)
-        halo_copy(h + 1).wait_recv()
-        for t in range(HALO):
-            value = xrecv[h + 1, t] + remote_part(h + 1, rows_far[t : t + 1, :])
-            adj[days + t] = jnp.where(has_next, value, 0.0)
+
+        @pl.when(has_next)
+        def _():
+            wait_bytes(far_msg.at[h, pl.ds(0, parts - 1)], rf.at[h])
+            unpack(h, far_msg, rows_far)
+            take_halo(h + 1)
+            for t in range(HALO):
+                adj[days + t] = xrecv[h + 1, t] + remote_part(h + 1, rows_far[t : t + 1, :])
 
     last = LEVELS - 1
     gradient(last)
@@ -322,13 +408,19 @@
 
     @pl.loop(0, LEVELS)
     def _(h):
-        wait_bytes(xsend.at[h, pl.ds(0, HALO)], sx.at[h])
         wait_bytes(precv.at[h], sp.at[h])
+
+        @pl.when(has_prev)
+        def _():
+            wait_bytes(xsend.at[h, pl.ds(0, HALO)], sx.at[h])
 
     @pl.loop(0, LEVELS - 1)
     def _(h):
         wait_bytes(out_msg.at[h, pl.ds(0, parts - 1)], so.at[h])
-        wait_bytes(out_msg.at[h, pl.ds(0, parts - 1)], sf.at[h])
+
+        @pl.when(has_prev)
+        def _():
+            wait_bytes(out_msg.at[h, pl.ds(0, parts - 1)], sf.at[h])
 
 
 def shards(parts, shifts, inflow, cotangent, gauge_reach, shape_param, scale_param, block_level, down_local, in_slot, send_reach):
@@ -343,6 +435,7 @@
     rounds = LEVELS - 1
     tile = (TILES, LANES)
     vmem = pl.BlockSpec(memory_space=pltpu.VMEM)
+    hbm = pl.BlockSpec(memory_space=pltpu.HBM)
     dma = pltpu.SemaphoreType.DMA
     return pl.pallas_call(
         functools.partial(adjoint_kernel, parts, shifts, days),
@@ -350,9 +443,18 @@
             jax.ShapeDtypeStruct((days, reaches), f32),
             jax.ShapeDtypeStruct((2, reaches), f32),
         ),
-        in_specs=[pl.BlockSpec(memory_space=pltpu.SMEM)] + [vmem] * 8,
+        in_specs=[pl.BlockSpec(memory_space=pltpu.SMEM)] + [hbm] * 8,
         out_specs=(vmem, vmem),
         scratch_shapes=[
+            pltpu.SMEM((LEVELS * MAXB + block_level.shape[0],), i32),
+            pltpu.VMEM((days, gauges), f32),
+            pltpu.VMEM((1, gauges), i32),
+            pltpu.VMEM((lines, LANES), f32),
+            pltpu.VMEM((lines, LANES), f32),
+            pltpu.VMEM((lines, LANES), i32),
+            pltpu.VMEM((lines, LANES), i32),
+            pltpu.VMEM(send.shape, i32),
+            dma((8,)),
             pltpu.VMEM((2 * days, gauges), jnp.bfloat16),
             pltpu.VMEM((1, gauges), i32),
             pltpu.VMEM((levels, days) + tile, f32),
@@ -390,10 +492,10 @@
             dma((levels,)),
         ],
         compiler_params=pltpu.CompilerParams(
-            has_side_effects=True, vmem_limit_bytes=40 * 1024 * 1024
+            collective_id=0, has_side_effects=True, vmem_limit_bytes=40 * 1024 * 1024
         ),
     )(
-        block_tables(block_level),
+        block_level,
         cotangent,
         gauge_reach.reshape(1, gauges),
         inflow,

time: 88.2 us -> 78.2 us (0.89)
  Pallas kernels: 78.9 us -> 69.5 us
  other arithmetic: 1.75 us -> 0 us
  local copies, waits for them, and re-layouts: 6.25 us -> 7.6 us
    pallas_call x1, Pallas kernels: 78.9 us -> 69.5 us  [shards(): pl.pallas_call(functools.partial(adjoint_kernel, parts, shifts, days), ou...]
    unnamed x17 -> x19, local copies, waits for them, and re-layouts: 6.25 us -> 7.6 us
    reduce_sum x2 -> x0, other arithmetic: 1 us -> none  [the longest x1 0.91 us: block_tables(): place = block_level * MAXB + jnp.sum(before.astype(jnp.int32), axis=1)]
where the time goes in v1:
time: 78.2 us; the launch traced here: 77.7 us
  Pallas kernels  69.5 us (89%)
  local copies, waits for them, and re-layouts  7.6 us (10%)
    pallas_call x1, Pallas kernels, shards(): pl.pallas_call(functools.partial(adjoint_kernel, parts, shifts, days), ou...  69.5 us
    unnamed x19, local copies, waits for them, and re-layouts  7.6 us

profile of v1, /device:TPU:1, one launch (start us, length us, event | category | flops | bytes accessed | tf_op | source)
XLA Modules:
  0.0 77.7 jit_solution(7449262115944205842)
XLA Ops:
  0.6 0.0 copy-start.2
  0.6 0.7 copy.13
  1.3 0.0 copy-start.7
  1.3 0.0 copy-done.2
  1.3 0.6 copy-done.7
  2.0 0.0 copy-start
  2.0 1.0 %copy-done = f32[32,4096]{1,0:T(8,128)S(1)} copy-done((f32[32,4096]{1,0:T(8,128)S(1)}, f32[32,4096]{1,0:T(8,128)}, u32[]{:S(2)}) %copy-start) | copy-done | bytes 524312
  3.0 0.0 copy-start.1
  3.0 0.9 %copy-done.1 = f32[32,2048]{1,0:T(8,128)S(1)} copy-done((f32[32,2048]{1,0:T(8,128)S(1)}, f32[32,2048]{1,0:T(8,128)}, u32[]{:S(2)}) %copy-start.1) | copy-done | bytes 262168
  4.0 0.0 copy-start.3
  4.0 0.7 copy-done.3
  4.7 0.0 copy-start.4
  4.7 0.7 copy-done.4
  5.4 0.0 copy-start.5
  5.4 0.7 copy-done.5
  6.1 0.0 copy-start.6
  6.1 0.7 copy-done.6
  6.8 69.5 %shard_map.104 = (f32[32,4096]{1,0:T(8,128)S(1)}, f32[2,4096]{1,0:T(2,128)S(1)}) custom-call(s32[16]{0:T(128)S(1)} %copy-done.7, f32[32,2048]{1,0:T(8,128)S(1)} %copy-done.1, s32[1,2048]{1,0:T(1,128)S(1)} %bitcast.13, f32[32,4096]{1,0:T(8,128)S(1)} %copy-done, f32[32,128]{1,0:T(8,128)S(1)} %bitcast.9, f32[32,128]{1,0:T(8,128)S(1)} %bitcast.10, ...), custom_call_target="tpu_custom_call" | custom-call | tf_op jit(solution)/shard_map/pallas_call | solution.py:440
  76.3 0.8 %copy.16 = f32[32,4096]{1,0:T(8,128)} copy(f32[32,4096]{1,0:T(8,128)S(1)} %get-tuple-element.4) | data formatting | bytes 1048576
  77.1 0.6 copy.17
Async XLA Ops:
  0.6 0.7 copy-start.2
  1.3 0.7 copy-start.7
  2.0 1.0 %copy-start = (f32[32,4096]{1,0:T(8,128)S(1)}, f32[32,4096]{1,0:T(8,128)}, u32[]{:S(2)}) copy-start(f32[32,4096]{1,0:T(8,128)} %inflow_h.1) | copy-start | bytes 1572868
  3.0 0.9 %copy-start.1 = (f32[32,2048]{1,0:T(8,128)S(1)}, f32[32,2048]{1,0:T(8,128)}, u32[]{:S(2)}) copy-start(f32[32,2048]{1,0:T(8,128)} %cot_h.1) | copy-start | bytes 786436
  4.0 0.7 copy-start.3
  4.7 0.7 copy-start.4
  5.4 0.7 copy-start.5
  6.1 0.7 copy-start.6

commit v2 on v1

--- a/solution.py
+++ b/solution.py
@@ -69,6 +69,9 @@
     lag_sum,
     psend,
     precv,
+    plast,
+    gsum,
+    gall,
     ptotal,
     lat_lv,
     staged,
@@ -87,6 +90,16 @@
     prev = lax.rem(shift + shifts - 1, shifts)
     has_next = shift < shifts - 1
     has_prev = shift > 0
+    side = max(1, math.isqrt(parts // 2))
+    hops = [min(d, side - d) for d in range(side)]
+    routes = [(y, x, c) for y in range(side) for x in range(side) for c in range(2)][1:]
+    routes.sort(key=lambda r: -(hops[r[0]] + hops[r[1]]))
+
+    def partner(route):
+        y = lax.rem(me // (2 * side) + route[0], side)
+        x = lax.rem(lax.rem(me // 2, side) + route[1], side)
+        return (y * side + x) * 2 + lax.rem(me + route[2], 2)
+
 
     def tile_of(reach):
         block = reach >> 8
@@ -163,17 +176,16 @@
         )
 
     def send_slots(h):
-        @pl.loop(1, parts)
-        def _(i):
-            q = lax.rem(me + i, parts)
-            slot_copy(h, q, shift, so, own_msg, ro).start()
-
         @pl.when(has_prev)
         def _():
-            @pl.loop(1, parts)
-            def _(i):
-                q = lax.rem(me + i, parts)
-                slot_copy(h, q, prev, sf, far_msg, rf).start()
+            for i in routes:
+                slot_copy(h, partner(i), prev, sf, far_msg, rf).start()
+                slot_copy(h, partner(i), shift, so, own_msg, ro).start()
+
+        @pl.when(jnp.logical_not(has_prev))
+        def _():
+            for i in routes:
+                slot_copy(h, partner(i), shift, so, own_msg, ro).start()
 
     def local_part(h):
         lane, tile = dlane[h], dtile[h]
@@ -237,13 +249,13 @@
             first = first + logit * LOGS[k]
             second = second + logit * OFFSETS[k]
         scl = scl_lv[h]
-        psend[h, 0] = first
-        psend[h, 1] = second / (scl * scl)
-
-    def grad_copy(h, i):
+        psend[h, :, 0, 0, :] = first
+        psend[h, :, 1, 0, :] = second / (scl * scl)
+
+    def peer_copy(src, dst, h, i):
         return pltpu.make_async_remote_copy(
-            src_ref=psend.at[h],
-            dst_ref=precv.at[h, i - 1],
+            src_ref=src,
+            dst_ref=dst,
             send_sem=sp.at[h],
             recv_sem=rp.at[h],
             device_id={"basin": me, "tm": lax.rem(shift + i, shifts)},
@@ -252,7 +264,8 @@
 
     def send_grads(h):
         for i in range(1, shifts):
-            grad_copy(h, i).start()
+            owner = lax.rem(shift + i, shifts)
+            peer_copy(psend.at[h, owner], precv.at[h, i - 1], h, i).start()
 
     def keep(h):
         for s in range(TILES):
@@ -337,11 +350,10 @@
     send_halo(0)
     for copy in loads[2:]:
         copy.wait()
-    wanted = jnp.maximum(send[...], 0)
-    wanted_tile = tile_of(wanted)[1]
     for h in range(LEVELS - 1):
-        wlane[h] = jnp.broadcast_to(wanted[h : h + 1, :] & (LANES - 1), (8, LANES))
-        wtile[h] = jnp.broadcast_to(wanted_tile[h : h + 1, :], (8, LANES))
+        wanted = jnp.broadcast_to(jnp.maximum(send[h], 0), (8, LANES))
+        wlane[h] = wanted & (LANES - 1)
+        wtile[h] = tile_of(wanted)[1]
     turn[...] = jnp.zeros_like(turn)
     pltpu.make_async_copy(staged, staged, load_sem.at[len(loads)]).wait()
     prepare(0)
@@ -382,22 +394,36 @@
 
     last = LEVELS - 1
     gradient(last)
-    send_grads(last)
+    for i in range(1, shifts):
+        peer_copy(psend.at[last], plast.at[i - 1], last, i).start()
+
+    @pl.loop(0, last)
+    def _(h):
+        wait_bytes(precv.at[h], rp.at[h])
+        total = psend[h, shift]
+        for i in range(shifts - 1):
+            total = total + precv[h, i]
+        gsum[h] = total
+
+    for i in range(1, shifts):
+        peer_copy(gsum, gall.at[shift], LEVELS, i).start()
+    gall[shift] = gsum[...]
     routed(last)
     keep(last)
     for b in range(blocks):
         place = table[LEVELS * MAXB + b]
         for j in range(2):
             lat[:, pl.ds(b * BLK + j * LANES, LANES)] = lat_lv[place * 2 + j]
-
-    @pl.loop(0, LEVELS)
-    def _(h):
-        wait_bytes(precv.at[h], rp.at[h])
-        total = psend[h]
+    wait_bytes(gall.at[pl.ds(0, shifts - 1)], rp.at[LEVELS])
+    for h in range(last):
+        for r in range(2):
+            ptotal[r, h * TILES : (h + 1) * TILES, :] = gall[:, h, r, 0, :]
+    wait_bytes(plast, rp.at[last])
+    for r in range(2):
+        total = psend[last, :, r, 0, :]
         for i in range(shifts - 1):
-            total = total + precv[h, i]
-        for r in range(2):
-            ptotal[r, pl.ds(pl.multiple_of(h * TILES, TILES), TILES), :] = total[r]
+            total = total + plast[i, :, r, 0, :]
+        ptotal[r, last * TILES : LEVELS * TILES, :] = total
 
     for b in range(blocks):
         place = table[LEVELS * MAXB + b]
@@ -408,7 +434,6 @@
 
     @pl.loop(0, LEVELS)
     def _(h):
-        wait_bytes(precv.at[h], sp.at[h])
 
         @pl.when(has_prev)
         def _():
@@ -417,19 +442,22 @@
     @pl.loop(0, LEVELS - 1)
     def _(h):
         wait_bytes(out_msg.at[h, pl.ds(0, parts - 1)], so.at[h])
+        wait_bytes(precv.at[h], sp.at[h])
 
         @pl.when(has_prev)
         def _():
             wait_bytes(out_msg.at[h, pl.ds(0, parts - 1)], sf.at[h])
+    wait_bytes(plast, sp.at[last])
+    wait_bytes(gall.at[pl.ds(0, shifts - 1)], sp.at[LEVELS])
 
 
 def shards(parts, shifts, inflow, cotangent, gauge_reach, shape_param, scale_param, block_level, down_local, in_slot, send_reach):
     days, reaches = inflow.shape
     gauges = cotangent.shape[1]
     lines = reaches // LANES
-    send = send_reach[0]
-    if send.shape[1] < LANES:
-        send = jnp.pad(send, ((0, 0), (0, LANES - send.shape[1])))
+    send = send_reach
+    if send.shape[2] < LANES:
+        send = jnp.pad(send, ((0, 0), (0, 0), (0, LANES - send.shape[2])))
     f32, i32 = jnp.float32, jnp.int32
     levels = LEVELS
     rounds = LEVELS - 1
@@ -453,7 +481,7 @@
             pltpu.VMEM((lines, LANES), f32),
             pltpu.VMEM((lines, LANES), i32),
             pltpu.VMEM((lines, LANES), i32),
-            pltpu.VMEM(send.shape, i32),
+            pltpu.VMEM((send.shape[1], 1, LANES), i32),
             dma((8,)),
             pltpu.VMEM((2 * days, gauges), jnp.bfloat16),
             pltpu.VMEM((1, gauges), i32),
@@ -477,8 +505,11 @@
             pltpu.VMEM((days, LANES), f32),
             pltpu.VMEM((days, LANES), f32),
             pltpu.VMEM((LAGS,) + tile, f32),
-            pltpu.VMEM((levels, 2) + tile, f32),
-            pltpu.VMEM((levels, shifts - 1, 2) + tile, f32),
+            pltpu.VMEM((levels, TILES, 2, 1, LANES), f32),
+            pltpu.VMEM((rounds, shifts - 1, 2, 1, LANES), f32),
+            pltpu.VMEM((shifts - 1, TILES, 2, 1, LANES), f32),
+            pltpu.VMEM((rounds, 2, 1, LANES), f32),
+            pltpu.VMEM((shifts, rounds, 2, 1, LANES), f32),
             pltpu.VMEM((2, levels * TILES, LANES), f32),
             pltpu.VMEM((levels * TILES, days, LANES), f32),
             pltpu.VMEM((lines, days, LANES), f32),
@@ -488,11 +519,11 @@
             dma((rounds,)),
             dma((rounds,)),
             dma((rounds,)),
-            dma((levels,)),
-            dma((levels,)),
+            dma((levels + 1,)),
+            dma((levels + 1,)),
         ],
         compiler_params=pltpu.CompilerParams(
-            collective_id=0, has_side_effects=True, vmem_limit_bytes=40 * 1024 * 1024
+            collective_id=0, has_side_effects=True, vmem_limit_bytes=66000000
         ),
     )(
         block_level,
@@ -503,7 +534,7 @@
         scale_param.reshape(lines, LANES),
         down_local.reshape(lines, LANES),
         in_slot.reshape(lines, LANES),
-        send,
+        jnp.transpose(send, (1, 0, 2)),
     )
 
 

time: 78.2 us -> 69.5 us (0.89)
  local copies, waits for them, and re-layouts: 7.6 us -> 2.49 us
  Pallas kernels: 69.5 us -> 66 us
    unnamed x19 -> x4, local copies, waits for them, and re-layouts: 7.6 us -> 2.49 us
    pallas_call x1, Pallas kernels: 69.5 us -> 66 us  [shards(): pl.pallas_call(functools.partial(adjoint_kernel, parts, shifts, days), ou...]
where the time goes in v2:
time: 69.5 us; the launch traced here: 69.1 us
  Pallas kernels  66 us (95%)
  local copies, waits for them, and re-layouts  2.49 us (4%)
    pallas_call x1, Pallas kernels, shards(): pl.pallas_call(functools.partial(adjoint_kernel, parts, shifts, days), ou...  66 us
    unnamed x4, local copies, waits for them, and re-layouts  2.49 us

profile of v2, /device:TPU:1, one launch (start us, length us, event | category | flops | bytes accessed | tf_op | source)
XLA Modules:
  0.0 69.1 jit_solution(7680867292931329956)
XLA Ops:
  0.6 66.0 %shard_map.104 = (f32[32,4096]{1,0:T(8,128)}, f32[2,4096]{1,0:T(2,128)}) custom-call(s32[16]{0:T(128)} %levels.1, f32[32,2048]{1,0:T(8,128)} %cot_h.1, s32[1,2048]{1,0:T(1,128)} %bitcast.10, f32[32,4096]{1,0:T(8,128)} %inflow_h.1, f32[32,128]{1,0:T(8,128)} %bitcast.6, f32[32,128]{1,0:T(8,128)} %bitcast.7, s32[32,128]{1,0:T(8,128)} %bitcast.8, ...), custom_call_target="tpu_custom_call" | custom-call | tf_op jit(solution)/shard_map/pallas_call | solution.py:468
  66.6 0.0 copy-start
  66.7 1.9 %copy.13 = f32[32,4096]{1,0:T(8,128)} copy(f32[32,4096]{1,0:T(8,128)} %get-tuple-element.4) | data formatting | bytes 1048576
  68.5 0.0 copy-done
  68.5 0.6 copy.14
Async XLA Ops:
  66.6 1.9 %copy-start = (f32[2,4096]{1,0:T(2,128)S(1)}, f32[2,4096]{1,0:T(2,128)}, u32[]{:S(2)}) copy-start(f32[2,4096]{1,0:T(2,128)} %get-tuple-element.5) | copy-start | bytes 98308

commit v3 on v2

--- a/solution.py
+++ b/solution.py
@@ -16,7 +16,6 @@
 LANES = 128
 TILES = MAXB * BLK // LANES
 HALO = LAGS - 1
-UNROLL = 32
 OFFSETS = [k + 0.5 for k in range(LAGS)]
 LOGS = [math.log(o) for o in OFFSETS]
 
@@ -142,11 +141,19 @@
             for j in range(width // LANES):
                 seed[h, :, 2 * c + j, :] = sums[:, j * LANES : (j + 1) * LANES]
 
-    def routed(h):
-        total = kern[h, 0][None] * adj[pl.ds(0, days)]
-        for k in range(1, LAGS):
-            total = total + kern[h, k][None] * adj[pl.ds(k, days)]
-        lday[...] = total
+    def routed_own(h):
+        for g in range(0, days, 8):
+            total = kern[h, 0][None] * adj[pl.ds(g, 8)]
+            for k in range(1, min(LAGS, days - 7 - g)):
+                total = total + kern[h, k][None] * adj[pl.ds(g + k, 8)]
+            lday[pl.ds(g, 8)] = total
+
+    def routed_far(h):
+        for g in range(0, days, 8):
+            total = lday[pl.ds(g, 8)]
+            for k in range(days - 7 - g, LAGS):
+                total = total + kern[h, k][None] * adj[pl.ds(g + k, 8)]
+            lday[pl.ds(g, 8)] = total
 
     def outgoing(h):
         lane, tile = wlane[h], wtile[h]
@@ -187,37 +194,35 @@
             for i in routes:
                 slot_copy(h, partner(i), shift, so, own_msg, ro).start()
 
-    def local_part(h):
+    def local_part(h, first, count):
         lane, tile = dlane[h], dtile[h]
         masks = [tile == s for s in range(TILES)]
-
-        @pl.loop(0, days, unroll=UNROLL)
-        def _(t):
+        for t in range(first, first + count):
             got = jnp.zeros((TILES, LANES), jnp.float32)
             for s in range(TILES):
                 line = jnp.broadcast_to(lday[t, s : s + 1, :], (TILES, LANES))
                 got = jnp.where(masks[s], jnp.take_along_axis(line, lane, axis=1), got)
             xsend[h, t] = seed[h, t] + got
 
-    def halo_copy(h):
+    def halo_copy(h, first, count):
         return pltpu.make_async_remote_copy(
-            src_ref=xsend.at[h, pl.ds(0, HALO)],
-            dst_ref=xrecv.at[h],
+            src_ref=xsend.at[h, pl.ds(first, count)],
+            dst_ref=xrecv.at[h, pl.ds(first, count)],
             send_sem=sx.at[h],
             recv_sem=rx.at[h],
             device_id={"basin": me, "tm": prev},
             device_id_type=pl.DeviceIdType.MESH,
         )
 
-    def send_halo(h):
+    def send_halo(h, first, count):
         @pl.when(has_prev)
         def _():
-            halo_copy(h).start()
+            halo_copy(h, first, count).start()
 
     def take_halo(h):
         @pl.when(has_next)
         def _():
-            halo_copy(h).wait_recv()
+            wait_bytes(xrecv.at[h], rx.at[h])
 
     def unpack(h, buf, rows):
         arrived = buf[h, :, 0, :]
@@ -293,22 +298,20 @@
             inflow_h.at[:, pl.ds(i * LANES, LANES)], staged.at[i], load_sem.at[len(loads)]
         ).start()
 
-    @pl.loop(1, parts)
-    def _(i):
-        greet(lax.rem(me + i, parts), shift)
+    everyone = routes + [(0, 0, 0)]
 
     @pl.when(has_prev)
     def _():
-        @pl.loop(0, parts)
-        def _(i):
-            greet(lax.rem(me + i, parts), prev)
+        for i in everyone:
+            greet(partner(i), prev)
 
     @pl.when(has_next)
     def _():
-        @pl.loop(0, parts)
-        def _(i):
-            greet(lax.rem(me + i, parts), shift + 1)
-
+        for i in everyone:
+            greet(partner(i), shift + 1)
+
+    for i in routes:
+        greet(partner(i), shift)
     for i in range(1, shifts):
         greet(me, lax.rem(shift + i, shifts))
 
@@ -321,13 +324,6 @@
         places.append(place)
         table[LEVELS * MAXB + b] = place
 
-    @pl.loop(0, LEVELS * MAXB)
-    def _(i):
-        block = jnp.int32(0)
-        for b in range(1, blocks):
-            block = block + jnp.where(places[b] == i, b, 0)
-        table[i] = block
-
     loads[0].wait()
     loads[1].wait()
     value = cot[...]
@@ -347,7 +343,15 @@
     greeted = parts - 1 + shifts - 1
     greeted = greeted + parts * (has_prev.astype(jnp.int32) + has_next.astype(jnp.int32))
     pl.semaphore_wait(barrier, greeted)
-    send_halo(0)
+    send_halo(0, 0, HALO)
+
+    @pl.loop(0, LEVELS * MAXB)
+    def _(i):
+        block = jnp.int32(0)
+        for b in range(1, blocks):
+            block = block + jnp.where(places[b] == i, b, 0)
+        table[i] = block
+
     for copy in loads[2:]:
         copy.wait()
     for h in range(LEVELS - 1):
@@ -359,17 +363,21 @@
     prepare(0)
     prepare(1)
     seeds(1)
+    adj[pl.ds(0, days)] = xsend[0]
+    routed_own(0)
     take_halo(0)
-    adj[pl.ds(0, days)] = xsend[0]
     adj[pl.ds(days, HALO)] = xrecv[0]
 
     @pl.loop(0, LEVELS - 1)
     def _(h):
-        routed(h)
+        routed_far(h)
         outgoing(h)
         send_slots(h)
-        local_part(h + 1)
-        send_halo(h + 1)
+        half = days // 2
+        local_part(h + 1, 0, half)
+        send_halo(h + 1, 0, half)
+        local_part(h + 1, half, days - half)
+        send_halo(h + 1, half, HALO - half)
         gradient(h)
         send_grads(h)
         keep(h)
@@ -383,6 +391,7 @@
         unpack(h, own_msg, rows_own)
         for t in range(days):
             adj[t] = xsend[h + 1, t] + remote_part(h + 1, rows_own[t : t + 1, :])
+        routed_own(h + 1)
 
         @pl.when(has_next)
         def _():
@@ -408,7 +417,7 @@
     for i in range(1, shifts):
         peer_copy(gsum, gall.at[shift], LEVELS, i).start()
     gall[shift] = gsum[...]
-    routed(last)
+    routed_far(last)
     keep(last)
     for b in range(blocks):
         place = table[LEVELS * MAXB + b]

time: 69.5 us -> 67.5 us (0.971)
  Pallas kernels: 66 us -> 64.2 us
    pallas_call x1, Pallas kernels: 66 us -> 64.2 us  [shards(): pl.pallas_call(functools.partial(adjoint_kernel, parts, shifts, days), ou...]
where the time goes in v3:
time: 67.5 us; the launch traced here: 67.3 us
  Pallas kernels  64.2 us (95%)
  local copies, waits for them, and re-layouts  2.49 us (4%)
    pallas_call x1, Pallas kernels, shards(): pl.pallas_call(functools.partial(adjoint_kernel, parts, shifts, days), ou...  64.2 us
    unnamed x4, local copies, waits for them, and re-layouts  2.49 us

profile of v3, /device:TPU:1, one launch (start us, length us, event | category | flops | bytes accessed | tf_op | source)
XLA Modules:
  0.0 67.3 jit_solution(15025413727712085984)
XLA Ops:
  0.6 64.2 %shard_map.104 = (f32[32,4096]{1,0:T(8,128)}, f32[2,4096]{1,0:T(2,128)}) custom-call(s32[16]{0:T(128)} %levels.1, f32[32,2048]{1,0:T(8,128)} %cot_h.1, s32[1,2048]{1,0:T(1,128)} %bitcast.10, f32[32,4096]{1,0:T(8,128)} %inflow_h.1, f32[32,128]{1,0:T(8,128)} %bitcast.6, f32[32,128]{1,0:T(8,128)} %bitcast.7, s32[32,128]{1,0:T(8,128)} %bitcast.8, ...), custom_call_target="tpu_custom_call" | custom-call | tf_op jit(solution)/shard_map/pallas_call | solution.py:477
  64.8 0.0 copy-start
  64.8 1.9 %copy.13 = f32[32,4096]{1,0:T(8,128)} copy(f32[32,4096]{1,0:T(8,128)} %get-tuple-element.4) | data formatting | bytes 1048576
  66.7 0.0 copy-done
  66.7 0.6 copy.14
Async XLA Ops:
  64.8 1.9 %copy-start = (f32[2,4096]{1,0:T(2,128)S(1)}, f32[2,4096]{1,0:T(2,128)}, u32[]{:S(2)}) copy-start(f32[2,4096]{1,0:T(2,128)} %get-tuple-element.5) | copy-start | bytes 98308

commit v4 on v3

--- a/solution.py
+++ b/solution.py
@@ -100,6 +100,8 @@
         return (y * side + x) * 2 + lax.rem(me + route[2], 2)
 
 
+    partners = [partner(route) for route in routes]
+
     def tile_of(reach):
         block = reach >> 8
         slot = jnp.zeros_like(reach)
@@ -185,14 +187,14 @@
     def send_slots(h):
         @pl.when(has_prev)
         def _():
-            for i in routes:
-                slot_copy(h, partner(i), prev, sf, far_msg, rf).start()
-                slot_copy(h, partner(i), shift, so, own_msg, ro).start()
+            for q in partners:
+                slot_copy(h, q, prev, sf, far_msg, rf).start()
+                slot_copy(h, q, shift, so, own_msg, ro).start()
 
         @pl.when(jnp.logical_not(has_prev))
         def _():
-            for i in routes:
-                slot_copy(h, partner(i), shift, so, own_msg, ro).start()
+            for q in partners:
+                slot_copy(h, q, shift, so, own_msg, ro).start()
 
     def local_part(h, first, count):
         lane, tile = dlane[h], dtile[h]
@@ -298,20 +300,20 @@
             inflow_h.at[:, pl.ds(i * LANES, LANES)], staged.at[i], load_sem.at[len(loads)]
         ).start()
 
-    everyone = routes + [(0, 0, 0)]
+    everyone = partners + [me]
 
     @pl.when(has_prev)
     def _():
-        for i in everyone:
-            greet(partner(i), prev)
+        for q in everyone:
+            greet(q, prev)
 
     @pl.when(has_next)
     def _():
-        for i in everyone:
-            greet(partner(i), shift + 1)
-
-    for i in routes:
-        greet(partner(i), shift)
+        for q in everyone:
+            greet(q, shift + 1)
+
+    for q in partners:
+        greet(q, shift)
     for i in range(1, shifts):
         greet(me, lax.rem(shift + i, shifts))
 
@@ -379,14 +381,14 @@
         local_part(h + 1, half, days - half)
         send_halo(h + 1, half, HALO - half)
         gradient(h)
+        keep(h)
+
+        @pl.when(h < LEVELS - 2)
+        def _():
+            seeds(h + 2)
+
+        prepare(jnp.minimum(h + 2, LEVELS - 1))
         send_grads(h)
-        keep(h)
-
-        @pl.when(h < LEVELS - 2)
-        def _():
-            seeds(h + 2)
-
-        prepare(jnp.minimum(h + 2, LEVELS - 1))
         wait_bytes(own_msg.at[h, pl.ds(0, parts - 1)], ro.at[h])
         unpack(h, own_msg, rows_own)
         for t in range(days):

time: 67.5 us -> 67.5 us (level)
  no operation moved by 1% of the time
where the time goes in v4:
time: 67.5 us; the launch traced here: 67.4 us
  Pallas kernels  64.2 us (95%)
  local copies, waits for them, and re-layouts  2.49 us (4%)
    pallas_call x1, Pallas kernels, shards(): pl.pallas_call(functools.partial(adjoint_kernel, parts, shifts, days), ou...  64.2 us
    unnamed x4, local copies, waits for them, and re-layouts  2.49 us

profile of v4, /device:TPU:1, one launch (start us, length us, event | category | flops | bytes accessed | tf_op | source)
XLA Modules:
  0.0 67.4 jit_solution(4073578790763213031)
XLA Ops:
  0.6 64.2 %shard_map.104 = (f32[32,4096]{1,0:T(8,128)}, f32[2,4096]{1,0:T(2,128)}) custom-call(s32[16]{0:T(128)} %levels.1, f32[32,2048]{1,0:T(8,128)} %cot_h.1, s32[1,2048]{1,0:T(1,128)} %bitcast.10, f32[32,4096]{1,0:T(8,128)} %inflow_h.1, f32[32,128]{1,0:T(8,128)} %bitcast.6, f32[32,128]{1,0:T(8,128)} %bitcast.7, s32[32,128]{1,0:T(8,128)} %bitcast.8, ...), custom_call_target="tpu_custom_call" | custom-call | tf_op jit(solution)/shard_map/pallas_call | solution.py:479
  64.9 0.0 copy-start
  64.9 1.9 %copy.13 = f32[32,4096]{1,0:T(8,128)} copy(f32[32,4096]{1,0:T(8,128)} %get-tuple-element.4) | data formatting | bytes 1048576
  66.8 0.0 copy-done
  66.8 0.6 copy.14
Async XLA Ops:
  64.9 1.9 %copy-start = (f32[2,4096]{1,0:T(2,128)S(1)}, f32[2,4096]{1,0:T(2,128)}, u32[]{:S(2)}) copy-start(f32[2,4096]{1,0:T(2,128)} %get-tuple-element.5) | copy-start | bytes 98308
